TPU v7x, 32 devices: a whole 2x2x4 slice. The times are simulated.
32 devices in a mesh: groups: 2 (over y), seq: 4 (over z), head: 2 (over x), rep: 2 (over core).
Axes of the slice: x: 2, y: 2, z: 4, core: 2. Of those that a mesh axis runs over, the one named last changes fastest.
Arguments:
- book_tokens: bfloat16 [16384, 1024], P(('groups', 'seq', 'rep')), parts along dimension 0, may hold values from -6 to 6
- norm_gain: float32 [1024], replicated, may hold values from 0.1 to 1.9
- query_weight: bfloat16 [1024, 1024], P(None, 'head'), may hold values from -0.1875 to 0.1875
- key_weight: bfloat16 [1024, 1024], P(None, 'head'), may hold values from -0.1875 to 0.1875
- value_weight: bfloat16 [1024, 1024], P(None, 'head'), may hold values from -0.1875 to 0.1875
- proj_weight: bfloat16 [1024, 4096], P(None, 'head'), may hold values from -0.75 to 0.75
- dual_gains: float32 [4, 1024], P(None, 'head'), may hold values from 0.1 to 1.9
- out_weight: bfloat16 [1024, 1024], P(None, 'head'), may hold values from -1.5 to 1.5
- span_bounds: int32 [128, 2], P('groups'), parts along dimension 0, may hold values from 0 to 8192, as said below
Outputs:
- attended: bfloat16 [16384, 1024], P(('groups', 'seq', 'rep'), 'head'), parts along dimension 0
- pooled: float32 [128, 1024], P(('groups', 'seq', 'rep'), 'head'), parts along dimension 0
There are 2 independent parts, one for each index of `groups`. A program takes and returns all parts, laid end to end along the dimension named above; an argument that names none is the same for every part. Nothing has to cross between parts.
Inputs may be any that keep to these rules, and one draw needn't show every extreme that they name: `span_bounds`: each span lies inside the book and holds 1 to 512 tokens; spans may intersect and come in any order; the longest holds exactly 512 tokens.
All inputs are finite; a program needn't handle non-finite values.
Results may differ from a plain program's by a relative error of at most 0.023.
Values may be sent and summed in bfloat16 or wider, within the bound.
No kernel may reach another device: no remote copies, remote signals or barrier semaphores. Data moves between devices by JAX's collectives and lax.ppermute only.
A program may use at most 64 MiB of HBM per device.

v0:
```python
import jax
import jax.numpy as jnp
from jax import lax
from jax.sharding import PartitionSpec as P

DH = 64
R = 256
SEG = 128
softcap = 5.0
epsilon = 1e-05


def with_halo(cells, sides, width):
    for axis, dim in sides:
        count = lax.axis_size(axis)
        ends = count - 1
        head = lax.slice_in_dim(cells, 0, width, axis=dim)
        tail = lax.slice_in_dim(cells, cells.shape[dim] - width, cells.shape[dim], axis=dim)
        cells = jnp.concatenate(
            [
                lax.ppermute(tail, axis, [(i, (i + 1) % count) for i in range(ends)]),
                cells,
                lax.ppermute(head, axis, [((i + 1) % count, i) for i in range(ends)]),
            ],
            axis=dim,
        )
    return cells


def normalize(values, gain_row):
    centre = jnp.mean(values, axis=-1, keepdims=True)
    spread = jnp.mean(jnp.square(values - centre), axis=-1, keepdims=True)
    return (values - centre) * lax.rsqrt(spread + epsilon) * gain_row


def capped(values):
    return softcap * jnp.tanh(values / softcap)


def finish(total_numer, gain_rows):
    land_keys = normalize(total_numer[:, :, :DH], gain_rows[2][:, None, :])
    land_values = normalize(total_numer[:, :, DH:], gain_rows[3][:, None, :])
    return jnp.concatenate([land_keys, land_values], axis=-1).astype(jnp.bfloat16)


def per_device(
    book_tokens,
    norm_gain,
    query_weight,
    key_weight,
    value_weight,
    proj_weight,
    dual_gains,
    out_weight,
    span_bounds,
):
    tok_rows = book_tokens.shape[0]
    seq_devices = lax.axis_size(("seq", "rep"))
    seq_index = lax.axis_index(("seq", "rep"))
    first_row = seq_index * tok_rows
    length = tok_rows * seq_devices
    head_local = query_weight.shape[1] // DH
    normed = normalize(book_tokens.astype(jnp.float32), norm_gain).astype(jnp.bfloat16)
    queries = jnp.dot(normed, query_weight, preferred_element_type=jnp.float32).astype(jnp.bfloat16)
    queries = queries.reshape(tok_rows, head_local, DH)
    key_raw = jnp.dot(normed, key_weight, preferred_element_type=jnp.float32).reshape(
        tok_rows, head_local, DH
    )
    value_raw = jnp.dot(normed, value_weight, preferred_element_type=jnp.float32).reshape(
        tok_rows, head_local, DH
    )
    gain_rows = dual_gains.reshape(4, head_local, DH)
    near_pairs = jnp.concatenate(
        [normalize(key_raw, gain_rows[0]), normalize(value_raw, gain_rows[1])], axis=-1
    )
    near_pairs = near_pairs.astype(jnp.bfloat16)
    raw_pairs = jnp.concatenate([key_raw, value_raw], axis=-1).astype(jnp.bfloat16)
    logits = jnp.dot(normed, proj_weight, preferred_element_type=jnp.float32)
    proj_weights = jnp.exp(capped(logits)).astype(jnp.bfloat16).reshape(tok_rows, head_local, R)
    numerator = jnp.einsum(
        "nhr,nhe->hre", proj_weights, raw_pairs, preferred_element_type=jnp.float32
    )
    flat_pairs = near_pairs.reshape(tok_rows, head_local * 2 * DH)
    padded = with_halo(flat_pairs, ((("seq", "rep"), 0),), SEG // 2)
    segments = tok_rows // SEG
    blocks = padded.reshape(segments + 1, SEG, head_local, 2 * DH)
    window = jnp.concatenate([blocks[:-1], blocks[1:]], axis=1)
    position = (
        first_row + jnp.arange(segments)[:, None] * SEG + jnp.arange(2 * SEG)[None, :] - SEG // 2
    )
    inside = (position >= 0) & (position < length)
    query_blocks = queries.reshape(segments, SEG, head_local, DH)
    near_scores = jnp.einsum(
        "sqhd,skhd->shqk", query_blocks, window[..., :DH], preferred_element_type=jnp.float32
    )
    near_exp = jnp.where(inside[:, None, None, :], jnp.exp(capped(near_scores * DH ** (-0.5))), 0.0)
    total_numer = lax.psum(numerator.astype(jnp.bfloat16), ("seq", "rep")).astype(jnp.float32)
    land_pairs = finish(total_numer, gain_rows)
    far_scores = jnp.einsum(
        "sqhd,hrd->shqr", query_blocks, land_pairs[..., :DH], preferred_element_type=jnp.float32
    )
    far_exp = jnp.exp(capped(far_scores * DH ** (-0.5)))
    summed = jnp.sum(near_exp, axis=-1, keepdims=True) + jnp.sum(far_exp, axis=-1, keepdims=True)
    near_probs = (near_exp / summed).astype(jnp.bfloat16)
    far_probs = (far_exp / summed).astype(jnp.bfloat16)
    output = jnp.einsum(
        "shqk,skhd->sqhd", near_probs, window[..., DH:], preferred_element_type=jnp.float32
    )
    output = output + jnp.einsum(
        "shqr,hrd->sqhd", far_probs, land_pairs[..., DH:], preferred_element_type=jnp.float32
    )
    heads_out = output.astype(jnp.bfloat16).reshape(tok_rows, head_local * DH)
    projected = jnp.dot(
        lax.all_gather(heads_out, "head", axis=1, tiled=True),
        out_weight,
        preferred_element_type=jnp.float32,
    )
    attended = projected.astype(jnp.bfloat16)
    span_start = span_bounds[:, 0]
    span_end = span_bounds[:, 1]
    position_rows = first_row + jnp.arange(tok_rows)
    member = (position_rows[None, :] >= span_start[:, None]) & (
        position_rows[None, :] < span_end[:, None]
    )
    partial_sums = jnp.dot(
        member.astype(jnp.bfloat16), attended, preferred_element_type=jnp.float32
    )
    own_sums = lax.psum_scatter(
        partial_sums.astype(jnp.bfloat16), ("seq", "rep"), scatter_dimension=0, tiled=True
    ).astype(jnp.float32)
    span_rows = own_sums.shape[0]
    own_bounds = lax.dynamic_slice_in_dim(span_bounds, seq_index * span_rows, span_rows, 0)
    own_counts = (own_bounds[:, 1] - own_bounds[:, 0]).astype(jnp.float32)
    pooled = own_sums / own_counts[:, None]
    return (attended, pooled)


def solution(mesh):
    placed = (
        P(("groups", "seq", "rep"), None),
        P(),
        P(None, "head"),
        P(None, "head"),
        P(None, "head"),
        P(None, "head"),
        P(None, "head"),
        P(None, "head"),
        P("groups", None),
    )
    return jax.shard_map(
        per_device,
        mesh=mesh,
        in_specs=placed,
        out_specs=(P(("groups", "seq", "rep"), "head"), P(("groups", "seq", "rep"), "head")),
        check_vma=False,
    )
```

profile of v0, /device:TPU:0, one launch (start us, length us, event | category | flops | bytes accessed | tf_op | source)
XLA Modules:
  0.0 200.5 jit_solution(12161471431930354215)
XLA Ops:
  7.2 2.1 %convert_reduce_fusion = f32[1024]{0:T(1024)S(1)} fusion(bf16[1024,1024]{1,0:T(8,128)(2,1)} %param.9), kind=kLoop, calls=%fused_computation.9 | loop fusion | flops 2096128 | bytes 2101248 | tf_op jit(solution)/shard_map/reduce_sum | solution.py:31
  10.9 2.3 %bitcast_convert_fusion = (bf16[1024,8,64]{0,2,1:T(8,128)(2,1)}, f32[1024,512]{0,1:T(8,128)S(1)}) fusion(bf16[1024,1024]{1,0:T(8,128)(2,1)S(1)} %fusion.6, bf16[1024,512]{1,0:T(8,128)(2,1)S(1)} %copy-done), kind=kOutput, calls=%fused_computation.34 | convolution fusion | flops 1074266112 | bytes 6291456 | tf_op jit(solution)/shard_map/dot_general | solution.py:69
  14.4 2.3 %bitcast_convert_fusion.1 = (bf16[1024,8,64]{0,2,1:T(8,128)(2,1)}, f32[1024,512]{0,1:T(8,128)S(1)}) fusion(bf16[1024,1024]{1,0:T(8,128)(2,1)S(1)} %fusion.6, bf16[1024,512]{1,0:T(8,128)(2,1)S(1)} %copy-done.15), kind=kOutput, calls=%fused_computation.37 | convolution fusion | flops 1074266112 | bytes 6291456 | tf_op jit(solution)/shard_map/dot_general | solution.py:66
  18.3 2.2 %multiply_multiply_fusion = (bf16[1024,8,64]{0,2,1:T(8,128)(2,1)S(1)}, bf16[1024,8,64]{0,2,1:T(8,128)(2,1)S(1)}) fusion(f32[1024,512]{0,1:T(8,128)S(1)} %get-tuple-element.17, f32[8,64]{1,0:T(8,128)S(1)} %mul.128, f32[1024,8]{0,1:T(8,128)S(1)} %add_rsqrt_fusion, f32[1024,8]{0,1:T(8,128)S(1)} %broadcast_multiply_fusion, f32[8,64]{1,0:T(8,128)S(1)} %mul.123, ...), kind=kLoop, calls=%fused_computation.40 | loop fusion | flops 4194304 | bytes 6426624 | tf_op jit(solution)/shard_map/mul | solution.py:33
  21.0 2.4 %collective-permute-start = (bf16[64,1024]{1,0:T(8,128)(2,1)S(1)}, bf16[64,1024]{1,0:T(8,128)(2,1)S(1)}, u32[]{:S(2)}, u32[]{:S(2)}) collective-permute-start(bf16[64,1024]{1,0:T(8,128)(2,1)S(1)} %copy.38), channel_id=1, source_target_pairs={{0,1},{1,4},{4,5},{5,8},{8,9},{9,12},{12,13},{2,3},{3,6},{6,7},{7,... | collective-permute-start | bytes 393224 | tf_op jit(solution)/shard_map/ppermute | solution.py:21
  24.2 1.5 collective-permute-start.1
  25.6 9.9 %exponential_convert_fusion = bf16[1024,2048]{1,0:T(8,128)(2,1)} fusion(bf16[1024,1024]{1,0:T(8,128)(2,1)} %copy-done.6, bf16[1024,2048]{1,0:T(8,128)(2,1)} %param.14), kind=kOutput, calls=%fused_computation.5 | convolution fusion | flops 4301258752 | bytes 10485760 | tf_op jit(solution)/shard_map/dot_general | solution.py:78
  35.6 6.5 %copy.58 = bf16[1024,2048]{0,1:T(8,128)(2,1)} copy(bf16[1024,2048]{1,0:T(8,128)(2,1)} %exponential_convert_fusion) | data formatting | bytes 8388608 | tf_op jit(solution)/shard_map/reshape | solution.py:79
  42.1 4.5 %fusion.23 = bf16[8,256,128]{2,1,0:T(8,128)(2,1)} fusion(bf16[1024,8,256]{0,2,1:T(8,128)(2,1)} %bitcast.78, bf16[1024,8,64]{0,2,1:T(8,128)(2,1)S(1)} %copy-done.17, bf16[1024,8,64]{0,2,1:T(8,128)(2,1)} %get-tuple-element.18), kind=kOutput, calls=%fused_computation.46 | convolution fusion | flops 541327360 | bytes 6815744 | tf_op jit(solution)/shard_map/nhr,nhe->hre/dot_general | solution.py:80
  46.9 2.6 %copy.39 = bf16[1024,1024]{1,0:T(8,128)(2,1)} copy(bf16[1024,1024]{0,1:T(8,128)(2,1)S(1)} %bitcast.75) | data formatting | bytes 4194304 | tf_op jit(solution)/shard_map/convert_element_type | solution.py:76
  49.5 3.1 %convolution_convert_fusion.1 = bf16[1024,512]{1,0:T(8,128)(2,1)S(1)} fusion(bf16[1024,1024]{1,0:T(8,128)(2,1)} %copy-done.6, bf16[1024,512]{1,0:T(8,128)(2,1)} %param.11), kind=kOutput, calls=%fused_computation.45 | convolution fusion | flops 1074266112 | bytes 4194304 | tf_op jit(solution)/shard_map/dot_general | solution.py:64
  52.6 2.1 %reshape.140 = bf16[8,128,8,64]{3,2,1,0:T(8,128)(2,1)} reshape(bf16[1024,512]{1,0:T(8,128)(2,1)S(1)} %convolution_convert_fusion.1) | data formatting | bytes 2097152 | tf_op jit(solution)/shard_map/reshape;reshape | solution.py:92
  54.7 2.4 %copy.45 = bf16[8,128,8,64]{1,3,2,0:T(8,128)(2,1)S(1)} copy(bf16[8,128,8,64]{3,2,1,0:T(8,128)(2,1)} %reshape.140) | data formatting | bytes 2097152 | tf_op jit(solution)/shard_map/reshape;reshape | solution.py:92
  57.4 1.9 fusion.15
  59.3 2.0 copy.64
  61.2 4.3 %copy.42 = bf16[8,128,8,128]{1,3,2,0:T(8,128)(2,1)} copy(bf16[8,128,8,128]{3,2,1,0:T(8,128)(2,1)} %bitcast.76) | data formatting | bytes 4194304 | tf_op jit(solution)/shard_map/slice | solution.py:87
  65.5 1.9 copy.65
  67.5 4.3 %copy.43 = bf16[8,128,8,128]{1,3,2,0:T(8,128)(2,1)} copy(bf16[8,128,8,128]{3,2,1,0:T(8,128)(2,1)} %bitcast.77) | data formatting | bytes 4194304 | tf_op jit(solution)/shard_map/slice | solution.py:87
  71.7 7.5 %fusion.1 = (f32[8,8,128]{2,1,0:T(8,128)S(1)}, f32[8,8,128,256]{3,2,1,0:T(8,128)}) fusion(pred[8,256]{1,0:T(8,128)(4,1)S(1)} %fusion.45, bf16[8,128,8,64]{1,3,2,0:T(8,128)(2,1)S(1)} %copy.45, bf16[8,128,8,128]{1,3,2,0:T(8,128)(2,1)} %copy.43, bf16[8,128,8,128]{1,3,2,0:T(8,128)(2,1)S(1)} %copy-done.7), kind=kOutput, calls=%fused_computation.7 | convolution fusion | flops 281010176 | bytes 13666304 | tf_op jit(solution)/shard_map/sqhd,skhd->shqk/dot_general | solution.py:93
  79.2 28.3 %all-reduce.2.cloned.1.call-done = bf16[8,256,128]{2,1,0:T(8,128)(2,1)} async-done(((bf16[8,256,128]{2,1,0:T(8,128)(2,1)}), bf16[8,256,128]{2,1,0:T(8,128)(2,1)}) %all-reduce.2.cloned.1.call-update) | async-done | bytes 524304 | tf_op jit(solution)/shard_map/psum | solution.py:97
  107.5 1.1 convert_element_type.57
  108.7 0.9 slice_reduce_fusion
  109.6 1.6 multiply_reduce_fusion.2
  111.2 3.9 %bitcast_reduce_fusion = (f32[8,8,128]{2,1,0:T(8,128)S(1)}, f32[8,256,8,128]{1,3,0,2:T(8,128)S(1)}) fusion(bf16[8,128,8,64]{1,3,2,0:T(8,128)(2,1)S(1)} %copy-done.10, f32[8,256,128]{2,1,0:T(8,128)S(1)} %convert_element_type.57, f32[8,64]{1,0:T(8,128)S(1)} %mul.138, f32[8,256]{1,0:T(8,128)S(1)} %add_rsqrt_fusion.3, f32[8,256]{1,0:T(8,128)S(1)} %get-tuple-element.25), kind=kOutput, calls=%fused_computation.1 | convolution fusion | flops 275243008 | bytes 10536960 | tf_op jit(solution)/shard_map/sqhd,hrd->shqr/dot_general | solution.py:99
  115.2 5.2 %fusion.8 = f32[8,64,8,128]{3,1,0,2:T(8,128)S(1)} fusion(f32[8,256,8,128]{1,3,0,2:T(8,128)S(1)} %get-tuple-element.23, f32[8,8,128]{2,1,0:T(8,128)S(1)} %add.118, f32[8,256,128]{2,1,0:T(8,128)S(1)} %convert_element_type.57, f32[8,64]{1,0:T(8,128)S(1)} %mul.144, f32[8,256]{1,0:T(8,128)S(1)} %add_rsqrt_fusion.2, f32[8,256]{1,0:T(8,128)S(1)} %get-tuple-element.24), kind=kOutput, calls=%fused_computation.19 | convolution fusion | flops 277348352 | bytes 11585536 | tf_op jit(solution)/shard_map/shqr,hrd->sqhd/dot_general | solution.py:109
  120.4 3.8 %fusion.20 = bf16[8,128,8,64]{1,3,2,0:T(8,128)(2,1)S(1)} fusion(f32[8,64,8,128]{3,1,0,2:T(8,128)S(1)} %fusion.8, f32[8,8,128,256]{3,2,1,0:T(8,128)S(1)} %bitcast.84, f32[8,8,128]{2,1,0:T(8,128)S(1)} %add.118, pred[8,256]{1,0:T(8,128)(4,1)S(1)} %fusion.45, bf16[8,128,8,128]{1,3,2,0:T(8,128)(2,1)S(1)} %copy-done.7, bf16[8,128,8,128]{1,3,2,0:T(8,128)(2,1)S(1)} %copy-done.8), kind=kOutput, calls=%fused_computation.33 | convolution fusion | flops 284164096 | bytes 15763456 | tf_op jit(solution)/shard_map/shqk,skhd->sqhd/dot_general | solution.py:106
  124.9 1.3 copy.68
  126.3 32.1 %all-gather.2.cloned.1.call-done = bf16[1024,1024]{0,1:T(8,128)(2,1)} async-done(((bf16[1024,512]{0,1:T(8,128)(2,1)}), bf16[1024,1024]{0,1:T(8,128)(2,1)}) %all-gather.2.cloned.1.call-update) | async-done | bytes 2097168 | tf_op jit(solution)/shard_map/all_gather | solution.py:114
  158.4 3.0 %convolution_convert_fusion = bf16[1024,512]{1,0:T(8,128)(2,1)S(1)} fusion(bf16[1024,1024]{0,1:T(8,128)(2,1)} %all-gather.2.cloned.1.call-done, bf16[1024,512]{1,0:T(8,128)(2,1)S(1)} %copy-done.16), kind=kOutput, calls=%fused_computation.44 | convolution fusion | flops 1074266112 | bytes 4194304 | tf_op jit(solution)/shard_map/dot_general | solution.py:113
  161.4 1.0 convolution_convert_fusion.2
  162.4 30.2 %reduce-scatter.2.cloned.1.call-done = bf16[8,512]{1,0:T(8,128)(2,1)} async-done(((bf16[64,512]{1,0:T(8,128)(2,1)}), bf16[8,512]{1,0:T(8,128)(2,1)}) %reduce-scatter.2.cloned.1.call-update) | async-done | bytes 8208 | tf_op jit(solution)/shard_map/reduce_scatter | solution.py:128
  192.6 1.4 convert_divide_fusion
  (81 shorter events, 7.1 us)
Async XLA Ops:
  7.2 3.7 %copy-start = (bf16[1024,512]{1,0:T(8,128)(2,1)S(1)}, bf16[1024,512]{1,0:T(8,128)(2,1)}, u32[]{:S(2)}) copy-start(bf16[1024,512]{1,0:T(8,128)(2,1)} %param.13) | copy-start | bytes 3145732
  7.2 2.3 %copy-start.2 = (bf16[1024,1024]{1,0:T(8,128)(2,1)S(1)}, bf16[1024,1024]{1,0:T(8,128)(2,1)}, u32[]{:S(2)}) copy-start(bf16[1024,1024]{1,0:T(8,128)(2,1)} %param.9) | copy-start | bytes 6291460
  7.2 3.0 %copy-start.13 = (f32[1024]{0:T(1024)S(1)}, f32[1024]{0:T(1024)}, u32[]{:S(2)}) copy-start(f32[1024]{0:T(1024)} %param.10) | copy-start | bytes 12292
  7.2 100.3 %all-reduce.2.cloned.1.call-start = ((), (), s32[]{:S(2)}) async-start(), calls=%async_computation.1 | async-start | bytes 1048576 | tf_op jit(solution)/shard_map/psum | solution.py:97
  10.9 2.9 %copy-start.6 = (bf16[1024,1024]{1,0:T(8,128)(2,1)}, bf16[1024,1024]{1,0:T(8,128)(2,1)S(1)}, u32[]{:S(2)}) copy-start(bf16[1024,1024]{1,0:T(8,128)(2,1)S(1)} %fusion.6) | copy-start | bytes 6291460
  13.2 1.2 copy-start.15
  16.7 1.4 copy-start.3
  16.7 1.4 copy-start.12
  21.0 36.3 %collective-permute-start = (bf16[64,1024]{1,0:T(8,128)(2,1)S(1)}, bf16[64,1024]{1,0:T(8,128)(2,1)S(1)}, u32[]{:S(2)}, u32[]{:S(2)}) collective-permute-start(bf16[64,1024]{1,0:T(8,128)(2,1)S(1)} %copy.38), channel_id=1, source_target_pairs={{0,1},{1,4},{4,5},{5,8},{8,9},{9,12},{12,13},{2,3},{3,6},{6,7},{7,... | collective-permute-start | bytes 393224 | tf_op jit(solution)/shard_map/ppermute | solution.py:21
  24.2 33.2 %collective-permute-start.1 = (bf16[64,1024]{1,0:T(8,128)(2,1)}, bf16[64,1024]{1,0:T(8,128)(2,1)S(1)}, u32[]{:S(2)}, u32[]{:S(2)}) collective-permute-start(bf16[64,1024]{1,0:T(8,128)(2,1)} %copy.40), channel_id=1, source_target_pairs={{1,0},{4,1},{5,4},{8,5},{9,8},{12,9},{13,12},{3,2},{6,3},{7,6},{10... | collective-permute-start | bytes 393224 | tf_op jit(solution)/shard_map/ppermute | solution.py:23
  35.6 6.5 %copy-start.17 = (bf16[1024,8,64]{0,2,1:T(8,128)(2,1)S(1)}, bf16[1024,8,64]{0,2,1:T(8,128)(2,1)}, u32[]{:S(2)}) copy-start(bf16[1024,8,64]{0,2,1:T(8,128)(2,1)} %get-tuple-element.16) | copy-start | bytes 3145732
  46.6 111.8 %all-gather.2.cloned.1.call-start = ((), (), s32[]{:S(2)}) async-start(), calls=%async_computation.2 | async-start | bytes 3145728 | tf_op jit(solution)/shard_map/all_gather | solution.py:114
  54.7 2.7 %copy-start.4 = (bf16[1024,1024]{1,0:T(8,128)(2,1)S(1)}, bf16[1024,1024]{1,0:T(8,128)(2,1)}, u32[]{:S(2)}) copy-start(bf16[1024,1024]{1,0:T(8,128)(2,1)} %copy.39) | copy-start | bytes 6291460
  57.1 14.6 %copy-start.9 = (bf16[8,128,8,64]{1,3,2,0:T(8,128)(2,1)}, bf16[8,128,8,64]{1,3,2,0:T(8,128)(2,1)S(1)}, u32[]{:S(2)}) copy-start(bf16[8,128,8,64]{1,3,2,0:T(8,128)(2,1)S(1)} %copy.45) | copy-start | bytes 3145732
  61.2 4.3 %copy-start.5 = (bf16[128,8,8,128]{3,1,2,0:T(8,128)(2,1)S(1)}, bf16[128,8,8,128]{3,1,2,0:T(8,128)(2,1)}, u32[]{:S(2)}) copy-start(bf16[128,8,8,128]{3,1,2,0:T(8,128)(2,1)} %get-tuple-element.11) | copy-start | bytes 6291460
  67.5 4.3 %copy-start.7 = (bf16[8,128,8,128]{1,3,2,0:T(8,128)(2,1)S(1)}, bf16[8,128,8,128]{1,3,2,0:T(8,128)(2,1)}, u32[]{:S(2)}) copy-start(bf16[8,128,8,128]{1,3,2,0:T(8,128)(2,1)} %copy.42) | copy-start | bytes 6291460
  108.6 2.5 %copy-start.10 = (bf16[8,128,8,64]{1,3,2,0:T(8,128)(2,1)S(1)}, bf16[8,128,8,64]{1,3,2,0:T(8,128)(2,1)}, u32[]{:S(2)}) copy-start(bf16[8,128,8,64]{1,3,2,0:T(8,128)(2,1)} %copy-done.9) | copy-start | bytes 3145732
  111.2 9.2 %slice-start = ((s8[8388608]{0:T(1024)(128)(4,1)}), s8[4194304]{0:T(1024)(128)(4,1)S(1)}, s32[]{:S(2)}) async-start(s8[8388608]{0:T(1024)(128)(4,1)} %bitcast.83), calls=%async_computation.4 | async-start | bytes 8388608
  115.2 5.2 %copy-start.8 = (bf16[8,128,8,128]{1,3,2,0:T(8,128)(2,1)S(1)}, bf16[8,128,8,128]{1,3,2,0:T(8,128)(2,1)}, u32[]{:S(2)}) copy-start(bf16[8,128,8,128]{1,3,2,0:T(8,128)(2,1)} %copy.43) | copy-start | bytes 6291460
  115.2 5.2 %slice-start.1 = ((s8[8388608]{0:T(1024)(128)(4,1)}), s8[4194304]{0:T(1024)(128)(4,1)S(1)}, s32[]{:S(2)}) async-start(s8[8388608]{0:T(1024)(128)(4,1)} %bitcast.83), calls=%async_computation.5 | async-start | bytes 8388608
  124.8 1.4 copy-start.14
  124.9 33.5 %copy-start.16 = (bf16[1024,512]{1,0:T(8,128)(2,1)S(1)}, bf16[1024,512]{1,0:T(8,128)(2,1)}, u32[]{:S(2)}) copy-start(bf16[1024,512]{1,0:T(8,128)(2,1)} %param.16) | copy-start | bytes 3145732
  126.1 66.4 %reduce-scatter.2.cloned.1.call-start = ((), (), s32[]{:S(2)}) async-start(), calls=%async_computation.3 | async-start | bytes 73728 | tf_op jit(solution)/shard_map/reduce_scatter | solution.py:128
  158.4 35.6 %copy-start.1 = (bf16[1024,512]{1,0:T(8,128)(2,1)S(1)}, bf16[1024,512]{1,0:T(8,128)(2,1)}, u32[]{:S(2)}) copy-start(bf16[1024,512]{1,0:T(8,128)(2,1)} %param.13) | copy-start | bytes 3145732
  161.4 32.6 %copy-start.11 = (bf16[1024,512]{1,0:T(8,128)(2,1)}, bf16[1024,512]{1,0:T(8,128)(2,1)S(1)}, u32[]{:S(2)}) copy-start(bf16[1024,512]{1,0:T(8,128)(2,1)S(1)} %convolution_convert_fusion) | copy-start | bytes 3145732
Sparse Core Ops, SparseCore 0:
  46.8 60.7 all-reduce.1
  126.3 32.0 all-gather.1
  162.5 30.0 reduce-scatter.1
where the time goes:
time: 201 us; the launch traced here: 200 us
  waiting for transfers between devices  90.6 us (45%)
  matrix products  46.4 us (23%)
  local copies, waits for them, and re-layouts  31.1 us (15%)
  between operations  14.2 us (7%)
  other arithmetic  14 us (7%)
  starting transfers between devices  4.17 us (2%)
    all_gather x1, waiting for transfers between devices, per_device(): lax.all_gather(heads_out, 'head', axis=1, tiled=True)  32.1 us
    reduce_scatter x1, waiting for transfers between devices, per_device(): lax.psum_scatter(partial_sums.astype(jnp.bfloat16), ('seq', 'rep'), scatt...  30.2 us
    psum x1, waiting for transfers between devices, per_device(): lax.psum(numerator.astype(jnp.bfloat16), ('seq', 'rep')).astype(jnp.float32)  28.3 us
    dot_general x1, matrix products, per_device(): logits = jnp.dot(normed, proj_weight, preferred_element_type=jnp.float32)  9.95 us
    slice x2, local copies, waits for them, and re-layouts, per_device(): window = jnp.concatenate([blocks[:-1], blocks[1:]], axis=1)  8.56 us
    dot_general x1, matrix products, per_device(): jnp.einsum('sqhd,skhd->shqk', query_blocks, window[..., :DH], preferred_e...  7.46 us
    unnamed x43, local copies, waits for them, and re-layouts  6.76 us
    reshape x1, local copies, waits for them, and re-layouts, per_device(): jnp.exp(capped(logits)).astype(jnp.bfloat16)  6.49 us
  transfers between devices with their start and end apart: 5, of which 3 were waited for; matrix products, arithmetic and copies ran while one was open for 27% of the time, Pallas kernels for 0%

commit v1 on v0

--- a/solution.py
+++ b/solution.py
@@ -8,6 +8,11 @@
 SEG = 128
 softcap = 5.0
 epsilon = 1e-05
+
+
+def by_each_axis(value, inner_axis, outer_axis):
+    partial = lax.psum(value, inner_axis)
+    return lax.psum(partial, outer_axis)
 
 
 def with_halo(cells, sides, width):
@@ -94,7 +99,7 @@
         "sqhd,skhd->shqk", query_blocks, window[..., :DH], preferred_element_type=jnp.float32
     )
     near_exp = jnp.where(inside[:, None, None, :], jnp.exp(capped(near_scores * DH ** (-0.5))), 0.0)
-    total_numer = lax.psum(numerator.astype(jnp.bfloat16), ("seq", "rep")).astype(jnp.float32)
+    total_numer = by_each_axis(numerator.astype(jnp.bfloat16), "rep", "seq").astype(jnp.float32)
     land_pairs = finish(total_numer, gain_rows)
     far_scores = jnp.einsum(
         "sqhd,hrd->shqr", query_blocks, land_pairs[..., :DH], preferred_element_type=jnp.float32

time: 201 us -> 209 us (1.040)
  waiting for transfers between devices: 90.6 us -> 98.7 us
    psum x1 -> x2, waiting for transfers between devices: 28.3 us -> 35.4 us  [the longest x1 35.4 us: by_each_axis(): return lax.psum(partial, outer_axis)]
  transfers between devices with their start and end apart: 5 -> 6, of which waited for: 3 -> 3; matrix products, arithmetic and copies ran while one was open for 27% -> 26% of each run, Pallas kernels for 0% -> 0%
where the time goes in v1:
time: 209 us
  waiting for transfers between devices  98.7 us (47%)
  matrix products  46.4 us (22%)
  local copies, waits for them, and re-layouts  31.1 us (15%)
  between operations  14.2 us (7%)
  other arithmetic  14 us (7%)
  starting transfers between devices  4.21 us (2%)
    psum x1, waiting for transfers between devices, by_each_axis(): return lax.psum(partial, outer_axis)  35.4 us
    all_gather x1, waiting for transfers between devices, per_device(): lax.all_gather(heads_out, 'head', axis=1, tiled=True)  33.1 us
    reduce_scatter x1, waiting for transfers between devices, per_device(): lax.psum_scatter(partial_sums.astype(jnp.bfloat16), ('seq', 'rep'), scatt...  30.2 us
    dot_general x1, matrix products, per_device(): logits = jnp.dot(normed, proj_weight, preferred_element_type=jnp.float32)  9.95 us
    slice x2, local copies, waits for them, and re-layouts, per_device(): window = jnp.concatenate([blocks[:-1], blocks[1:]], axis=1)  8.57 us
    dot_general x1, matrix products, per_device(): jnp.einsum('sqhd,skhd->shqk', query_blocks, window[..., :DH], preferred_e...  7.45 us
    unnamed x43, local copies, waits for them, and re-layouts  6.76 us
    reshape x1, local copies, waits for them, and re-layouts, per_device(): jnp.exp(capped(logits)).astype(jnp.bfloat16)  6.49 us
  transfers between devices with their start and end apart: 6, of which 3 were waited for; matrix products, arithmetic and copies ran while one was open for 26% of the time, Pallas kernels for 0%

profile of v1, /device:TPU:0, one launch (start us, length us, event | category | flops | bytes accessed | tf_op | source)
XLA Modules:
  0.0 208.6 jit_solution(6272047725489434920)
XLA Ops:
  7.2 2.1 convert_reduce_fusion
  10.9 2.3 %bitcast_convert_fusion = (bf16[1024,8,64]{0,2,1:T(8,128)(2,1)}, f32[1024,512]{0,1:T(8,128)S(1)}) fusion(bf16[1024,1024]{1,0:T(8,128)(2,1)S(1)} %fusion.6, bf16[1024,512]{1,0:T(8,128)(2,1)S(1)} %copy-done), kind=kOutput, calls=%fused_computation.34 | convolution fusion | flops 1074266112 | bytes 6291456 | tf_op jit(solution)/shard_map/dot_general | solution.py:74
  14.4 2.3 %bitcast_convert_fusion.1 = (bf16[1024,8,64]{0,2,1:T(8,128)(2,1)}, f32[1024,512]{0,1:T(8,128)S(1)}) fusion(bf16[1024,1024]{1,0:T(8,128)(2,1)S(1)} %fusion.6, bf16[1024,512]{1,0:T(8,128)(2,1)S(1)} %copy-done.15), kind=kOutput, calls=%fused_computation.37 | convolution fusion | flops 1074266112 | bytes 6291456 | tf_op jit(solution)/shard_map/dot_general | solution.py:71
  18.3 2.2 %multiply_multiply_fusion = (bf16[1024,8,64]{0,2,1:T(8,128)(2,1)S(1)}, bf16[1024,8,64]{0,2,1:T(8,128)(2,1)S(1)}) fusion(f32[1024,512]{0,1:T(8,128)S(1)} %get-tuple-element.17, f32[8,64]{1,0:T(8,128)S(1)} %mul.128, f32[1024,8]{0,1:T(8,128)S(1)} %add_rsqrt_fusion, f32[1024,8]{0,1:T(8,128)S(1)} %broadcast_multiply_fusion, f32[8,64]{1,0:T(8,128)S(1)} %mul.123, ...), kind=kLoop, calls=%fused_computation.40 | loop fusion | flops 4194304 | bytes 6426624 | tf_op jit(solution)/shard_map/mul | solution.py:38
  21.0 2.4 %collective-permute-start = (bf16[64,1024]{1,0:T(8,128)(2,1)S(1)}, bf16[64,1024]{1,0:T(8,128)(2,1)S(1)}, u32[]{:S(2)}, u32[]{:S(2)}) collective-permute-start(bf16[64,1024]{1,0:T(8,128)(2,1)S(1)} %copy.38), channel_id=1, source_target_pairs={{0,1},{1,4},{4,5},{5,8},{8,9},{9,12},{12,13},{2,3},{3,6},{6,7},{7,... | collective-permute-start | bytes 393224 | tf_op jit(solution)/shard_map/ppermute | solution.py:26
  24.2 1.5 collective-permute-start.1
  25.7 10.0 %exponential_convert_fusion = bf16[1024,2048]{1,0:T(8,128)(2,1)} fusion(bf16[1024,1024]{1,0:T(8,128)(2,1)} %copy-done.6, bf16[1024,2048]{1,0:T(8,128)(2,1)} %param.14), kind=kOutput, calls=%fused_computation.5 | convolution fusion | flops 4301258752 | bytes 10485760 | tf_op jit(solution)/shard_map/dot_general | solution.py:83
  35.6 6.5 %copy.58 = bf16[1024,2048]{0,1:T(8,128)(2,1)} copy(bf16[1024,2048]{1,0:T(8,128)(2,1)} %exponential_convert_fusion) | data formatting | bytes 8388608 | tf_op jit(solution)/shard_map/reshape | solution.py:84
  42.1 4.5 %fusion.23 = bf16[8,256,128]{2,1,0:T(8,128)(2,1)} fusion(bf16[1024,8,256]{0,2,1:T(8,128)(2,1)} %bitcast.78, bf16[1024,8,64]{0,2,1:T(8,128)(2,1)S(1)} %copy-done.17, bf16[1024,8,64]{0,2,1:T(8,128)(2,1)} %get-tuple-element.18), kind=kOutput, calls=%fused_computation.46 | convolution fusion | flops 541327360 | bytes 6815744 | tf_op jit(solution)/shard_map/nhr,nhe->hre/dot_general | solution.py:85
  46.7 2.6 %copy.39 = bf16[1024,1024]{1,0:T(8,128)(2,1)} copy(bf16[1024,1024]{0,1:T(8,128)(2,1)S(1)} %bitcast.75) | data formatting | bytes 4194304 | tf_op jit(solution)/shard_map/convert_element_type | solution.py:81
  49.3 3.1 %convolution_convert_fusion.1 = bf16[1024,512]{1,0:T(8,128)(2,1)S(1)} fusion(bf16[1024,1024]{1,0:T(8,128)(2,1)} %copy-done.6, bf16[1024,512]{1,0:T(8,128)(2,1)} %param.11), kind=kOutput, calls=%fused_computation.45 | convolution fusion | flops 1074266112 | bytes 4194304 | tf_op jit(solution)/shard_map/dot_general | solution.py:69
  52.4 2.1 reshape.140
  54.5 2.4 %copy.45 = bf16[8,128,8,64]{1,3,2,0:T(8,128)(2,1)S(1)} copy(bf16[8,128,8,64]{3,2,1,0:T(8,128)(2,1)} %reshape.140) | data formatting | bytes 2097152 | tf_op jit(solution)/shard_map/reshape;reshape | solution.py:97
  57.2 1.9 fusion.15
  59.1 2.0 copy.64
  61.0 4.3 %copy.42 = bf16[8,128,8,128]{1,3,2,0:T(8,128)(2,1)} copy(bf16[8,128,8,128]{3,2,1,0:T(8,128)(2,1)} %bitcast.76) | data formatting | bytes 4194304 | tf_op jit(solution)/shard_map/slice | solution.py:92
  65.3 1.9 copy.65
  67.3 4.3 %copy.43 = bf16[8,128,8,128]{1,3,2,0:T(8,128)(2,1)} copy(bf16[8,128,8,128]{3,2,1,0:T(8,128)(2,1)} %bitcast.77) | data formatting | bytes 4194304 | tf_op jit(solution)/shard_map/slice | solution.py:92
  71.9 7.5 %fusion.1 = (f32[8,8,128]{2,1,0:T(8,128)S(1)}, f32[8,8,128,256]{3,2,1,0:T(8,128)}) fusion(pred[8,256]{1,0:T(8,128)(4,1)S(1)} %fusion.45, bf16[8,128,8,64]{1,3,2,0:T(8,128)(2,1)S(1)} %copy.45, bf16[8,128,8,128]{1,3,2,0:T(8,128)(2,1)} %copy.43, bf16[8,128,8,128]{1,3,2,0:T(8,128)(2,1)S(1)} %copy-done.7), kind=kOutput, calls=%fused_computation.7 | convolution fusion | flops 281010176 | bytes 13666304 | tf_op jit(solution)/shard_map/sqhd,skhd->shqk/dot_general | solution.py:98
  79.3 35.4 %all-reduce.5.cloned.1.call-done = bf16[8,256,128]{2,1,0:T(8,128)(2,1)} async-done(((bf16[8,256,128]{2,1,0:T(8,128)(2,1)}), bf16[8,256,128]{2,1,0:T(8,128)(2,1)}) %all-reduce.5.cloned.1.call-update) | async-done | bytes 524304 | tf_op jit(solution)/shard_map/psum | solution.py:15
  114.7 1.1 convert_element_type.57
  115.8 0.9 slice_reduce_fusion
  116.7 1.6 multiply_reduce_fusion.2
  118.3 3.9 %bitcast_reduce_fusion = (f32[8,8,128]{2,1,0:T(8,128)S(1)}, f32[8,256,8,128]{1,3,0,2:T(8,128)S(1)}) fusion(bf16[8,128,8,64]{1,3,2,0:T(8,128)(2,1)S(1)} %copy-done.10, f32[8,256,128]{2,1,0:T(8,128)S(1)} %convert_element_type.57, f32[8,64]{1,0:T(8,128)S(1)} %mul.138, f32[8,256]{1,0:T(8,128)S(1)} %add_rsqrt_fusion.3, f32[8,256]{1,0:T(8,128)S(1)} %get-tuple-element.25), kind=kOutput, calls=%fused_computation.1 | convolution fusion | flops 275243008 | bytes 10536960 | tf_op jit(solution)/shard_map/sqhd,hrd->shqr/dot_general | solution.py:104
  122.3 5.2 %fusion.8 = f32[8,64,8,128]{3,1,0,2:T(8,128)S(1)} fusion(f32[8,256,8,128]{1,3,0,2:T(8,128)S(1)} %get-tuple-element.23, f32[8,8,128]{2,1,0:T(8,128)S(1)} %add.120, f32[8,256,128]{2,1,0:T(8,128)S(1)} %convert_element_type.57, f32[8,64]{1,0:T(8,128)S(1)} %mul.144, f32[8,256]{1,0:T(8,128)S(1)} %add_rsqrt_fusion.2, f32[8,256]{1,0:T(8,128)S(1)} %get-tuple-element.24), kind=kOutput, calls=%fused_computation.19 | convolution fusion | flops 277348352 | bytes 11585536 | tf_op jit(solution)/shard_map/shqr,hrd->sqhd/dot_general | solution.py:114
  127.5 3.8 %fusion.20 = bf16[8,128,8,64]{1,3,2,0:T(8,128)(2,1)S(1)} fusion(f32[8,64,8,128]{3,1,0,2:T(8,128)S(1)} %fusion.8, f32[8,8,128,256]{3,2,1,0:T(8,128)S(1)} %bitcast.84, f32[8,8,128]{2,1,0:T(8,128)S(1)} %add.120, pred[8,256]{1,0:T(8,128)(4,1)S(1)} %fusion.45, bf16[8,128,8,128]{1,3,2,0:T(8,128)(2,1)S(1)} %copy-done.7, bf16[8,128,8,128]{1,3,2,0:T(8,128)(2,1)S(1)} %copy-done.8), kind=kOutput, calls=%fused_computation.33 | convolution fusion | flops 284164096 | bytes 15763456 | tf_op jit(solution)/shard_map/shqk,skhd->sqhd/dot_general | solution.py:111
  132.0 1.3 copy.68
  133.4 33.1 %all-gather.2.cloned.1.call-done = bf16[1024,1024]{0,1:T(8,128)(2,1)} async-done(((bf16[1024,512]{0,1:T(8,128)(2,1)}), bf16[1024,1024]{0,1:T(8,128)(2,1)}) %all-gather.2.cloned.1.call-update) | async-done | bytes 2097168 | tf_op jit(solution)/shard_map/all_gather | solution.py:119
  166.5 3.0 %convolution_convert_fusion = bf16[1024,512]{1,0:T(8,128)(2,1)S(1)} fusion(bf16[1024,1024]{0,1:T(8,128)(2,1)} %all-gather.2.cloned.1.call-done, bf16[1024,512]{1,0:T(8,128)(2,1)S(1)} %copy-done.16), kind=kOutput, calls=%fused_computation.44 | convolution fusion | flops 1074266112 | bytes 4194304 | tf_op jit(solution)/shard_map/dot_general | solution.py:118
  169.5 1.0 convolution_convert_fusion.2
  170.5 30.2 %reduce-scatter.2.cloned.1.call-done = bf16[8,512]{1,0:T(8,128)(2,1)} async-done(((bf16[64,512]{1,0:T(8,128)(2,1)}), bf16[8,512]{1,0:T(8,128)(2,1)}) %reduce-scatter.2.cloned.1.call-update) | async-done | bytes 8208 | tf_op jit(solution)/shard_map/reduce_scatter | solution.py:133
  200.7 1.4 convert_divide_fusion
  (84 shorter events, 7.2 us)
Async XLA Ops:
  7.2 3.7 %copy-start = (bf16[1024,512]{1,0:T(8,128)(2,1)S(1)}, bf16[1024,512]{1,0:T(8,128)(2,1)}, u32[]{:S(2)}) copy-start(bf16[1024,512]{1,0:T(8,128)(2,1)} %param.13) | copy-start | bytes 3145732
  7.2 2.3 %copy-start.2 = (bf16[1024,1024]{1,0:T(8,128)(2,1)S(1)}, bf16[1024,1024]{1,0:T(8,128)(2,1)}, u32[]{:S(2)}) copy-start(bf16[1024,1024]{1,0:T(8,128)(2,1)} %param.9) | copy-start | bytes 6291460
  7.2 3.0 %copy-start.13 = (f32[1024]{0:T(1024)S(1)}, f32[1024]{0:T(1024)}, u32[]{:S(2)}) copy-start(f32[1024]{0:T(1024)} %param.10) | copy-start | bytes 12292
  7.2 64.3 %all-reduce.3.cloned.1.call-start = ((), (), s32[]{:S(2)}) async-start(), calls=%async_computation.1 | async-start | bytes 1048576 | tf_op jit(solution)/shard_map/psum | solution.py:14
  10.9 2.9 %copy-start.6 = (bf16[1024,1024]{1,0:T(8,128)(2,1)}, bf16[1024,1024]{1,0:T(8,128)(2,1)S(1)}, u32[]{:S(2)}) copy-start(bf16[1024,1024]{1,0:T(8,128)(2,1)S(1)} %fusion.6) | copy-start | bytes 6291460
  13.2 1.2 copy-start.15
  16.7 1.4 copy-start.3
  16.7 1.4 copy-start.12
  21.0 36.1 %collective-permute-start = (bf16[64,1024]{1,0:T(8,128)(2,1)S(1)}, bf16[64,1024]{1,0:T(8,128)(2,1)S(1)}, u32[]{:S(2)}, u32[]{:S(2)}) collective-permute-start(bf16[64,1024]{1,0:T(8,128)(2,1)S(1)} %copy.38), channel_id=1, source_target_pairs={{0,1},{1,4},{4,5},{5,8},{8,9},{9,12},{12,13},{2,3},{3,6},{6,7},{7,... | collective-permute-start | bytes 393224 | tf_op jit(solution)/shard_map/ppermute | solution.py:26
  24.2 33.0 %collective-permute-start.1 = (bf16[64,1024]{1,0:T(8,128)(2,1)}, bf16[64,1024]{1,0:T(8,128)(2,1)S(1)}, u32[]{:S(2)}, u32[]{:S(2)}) collective-permute-start(bf16[64,1024]{1,0:T(8,128)(2,1)} %copy.40), channel_id=1, source_target_pairs={{1,0},{4,1},{5,4},{8,5},{9,8},{12,9},{13,12},{3,2},{6,3},{7,6},{10... | collective-permute-start | bytes 393224 | tf_op jit(solution)/shard_map/ppermute | solution.py:28
  35.6 6.5 %copy-start.17 = (bf16[1024,8,64]{0,2,1:T(8,128)(2,1)S(1)}, bf16[1024,8,64]{0,2,1:T(8,128)(2,1)}, u32[]{:S(2)}) copy-start(bf16[1024,8,64]{0,2,1:T(8,128)(2,1)} %get-tuple-element.16) | copy-start | bytes 3145732
  46.7 68.0 %all-reduce.5.cloned.1.call-start = ((), (), s32[]{:S(2)}) async-start(), calls=%async_computation.2 | async-start | bytes 1048576 | tf_op jit(solution)/shard_map/psum | solution.py:15
  54.5 2.7 %copy-start.4 = (bf16[1024,1024]{1,0:T(8,128)(2,1)S(1)}, bf16[1024,1024]{1,0:T(8,128)(2,1)}, u32[]{:S(2)}) copy-start(bf16[1024,1024]{1,0:T(8,128)(2,1)} %copy.39) | copy-start | bytes 6291460
  56.9 14.9 %copy-start.9 = (bf16[8,128,8,64]{1,3,2,0:T(8,128)(2,1)}, bf16[8,128,8,64]{1,3,2,0:T(8,128)(2,1)S(1)}, u32[]{:S(2)}) copy-start(bf16[8,128,8,64]{1,3,2,0:T(8,128)(2,1)S(1)} %copy.45) | copy-start | bytes 3145732
  61.0 4.3 %copy-start.5 = (bf16[128,8,8,128]{3,1,2,0:T(8,128)(2,1)S(1)}, bf16[128,8,8,128]{3,1,2,0:T(8,128)(2,1)}, u32[]{:S(2)}) copy-start(bf16[128,8,8,128]{3,1,2,0:T(8,128)(2,1)} %get-tuple-element.11) | copy-start | bytes 6291460
  67.2 4.6 %copy-start.7 = (bf16[8,128,8,128]{1,3,2,0:T(8,128)(2,1)S(1)}, bf16[8,128,8,128]{1,3,2,0:T(8,128)(2,1)}, u32[]{:S(2)}) copy-start(bf16[8,128,8,128]{1,3,2,0:T(8,128)(2,1)} %copy.42) | copy-start | bytes 6291460
  71.6 95.0 %all-gather.2.cloned.1.call-start = ((), (), s32[]{:S(2)}) async-start(), calls=%async_computation.3 | async-start | bytes 3145728 | tf_op jit(solution)/shard_map/all_gather | solution.py:119
  115.8 2.5 %copy-start.10 = (bf16[8,128,8,64]{1,3,2,0:T(8,128)(2,1)S(1)}, bf16[8,128,8,64]{1,3,2,0:T(8,128)(2,1)}, u32[]{:S(2)}) copy-start(bf16[8,128,8,64]{1,3,2,0:T(8,128)(2,1)} %copy-done.9) | copy-start | bytes 3145732
  118.3 9.2 %slice-start = ((s8[8388608]{0:T(1024)(128)(4,1)}), s8[4194304]{0:T(1024)(128)(4,1)S(1)}, s32[]{:S(2)}) async-start(s8[8388608]{0:T(1024)(128)(4,1)} %bitcast.83), calls=%async_computation.5 | async-start | bytes 8388608
  122.3 5.2 %copy-start.8 = (bf16[8,128,8,128]{1,3,2,0:T(8,128)(2,1)S(1)}, bf16[8,128,8,128]{1,3,2,0:T(8,128)(2,1)}, u32[]{:S(2)}) copy-start(bf16[8,128,8,128]{1,3,2,0:T(8,128)(2,1)} %copy.43) | copy-start | bytes 6291460
  122.3 5.2 %slice-start.1 = ((s8[8388608]{0:T(1024)(128)(4,1)}), s8[4194304]{0:T(1024)(128)(4,1)S(1)}, s32[]{:S(2)}) async-start(s8[8388608]{0:T(1024)(128)(4,1)} %bitcast.83), calls=%async_computation.6 | async-start | bytes 8388608
  132.0 1.4 copy-start.14
  132.0 34.5 %copy-start.16 = (bf16[1024,512]{1,0:T(8,128)(2,1)S(1)}, bf16[1024,512]{1,0:T(8,128)(2,1)}, u32[]{:S(2)}) copy-start(bf16[1024,512]{1,0:T(8,128)(2,1)} %param.16) | copy-start | bytes 3145732
  133.3 67.4 %reduce-scatter.2.cloned.1.call-start = ((), (), s32[]{:S(2)}) async-start(), calls=%async_computation.4 | async-start | bytes 73728 | tf_op jit(solution)/shard_map/reduce_scatter | solution.py:133
  166.5 35.6 %copy-start.1 = (bf16[1024,512]{1,0:T(8,128)(2,1)S(1)}, bf16[1024,512]{1,0:T(8,128)(2,1)}, u32[]{:S(2)}) copy-start(bf16[1024,512]{1,0:T(8,128)(2,1)} %param.13) | copy-start | bytes 3145732
  169.5 32.6 %copy-start.11 = (bf16[1024,512]{1,0:T(8,128)(2,1)}, bf16[1024,512]{1,0:T(8,128)(2,1)S(1)}, u32[]{:S(2)}) copy-start(bf16[1024,512]{1,0:T(8,128)(2,1)S(1)} %convolution_convert_fusion) | copy-start | bytes 3145732
Sparse Core Ops, SparseCore 0:
  46.8 23.3 all-reduce.2
  72.6 41.9 all-reduce.4
  133.4 33.0 all-gather.1
  170.7 30.0 reduce-scatter.1
